TPU v7x, 32 devices: a whole 2x2x4 slice. The times are simulated.
32 devices in a mesh: dp: 4 (over x, core), fsdp: 8 (over z, y).
Axes of the slice: x: 2, y: 2, z: 4, core: 2. Of those that a mesh axis runs over, the one named last changes fastest.
Arguments:
- tokens: bfloat16 [4, 1024, 768], P('dp', 'fsdp'), may hold values from -6 to 6
- ln1_gain: bfloat16 [768], P('fsdp'), may hold values from 0.099609375 to 1.8984375
- ln1_bias: bfloat16 [768], P('fsdp'), may hold values from -1.75 to 1.75
- ln2_gain: bfloat16 [768], P('fsdp'), may hold values from 0.099609375 to 1.8984375
- ln2_bias: bfloat16 [768], P('fsdp'), may hold values from -1.75 to 1.75
- qkv_weight: bfloat16 [768, 2304], P('fsdp'), may hold values from -0.21875 to 0.21875
- qkv_bias: bfloat16 [2304], P('fsdp'), may hold values from -3 to 3
- out_weight: bfloat16 [768, 768], P('fsdp'), may hold values from -1.75 to 1.75
- out_bias: bfloat16 [768], P('fsdp'), may hold values from -3 to 3
- up_weight: bfloat16 [768, 3072], P('fsdp'), may hold values from -0.21875 to 0.21875
- up_bias: bfloat16 [3072], P('fsdp'), may hold values from -3 to 3
- down_weight: bfloat16 [3072, 768], P('fsdp'), may hold values from -0.109375 to 0.109375
- down_bias: bfloat16 [768], P('fsdp'), may hold values from -3 to 3
- cotangent: bfloat16 [4, 1024, 768], P('dp', 'fsdp'), may hold values from -6 to 6
Outputs:
- layer_output: bfloat16 [4, 1024, 768], P('dp', 'fsdp')
- input_grad: float32 [4, 1024, 768], P('dp', 'fsdp')
- grad_ln1_gain: float32 [768], P('fsdp')
- grad_ln1_bias: float32 [768], P('fsdp')
- grad_ln2_gain: float32 [768], P('fsdp')
- grad_ln2_bias: float32 [768], P('fsdp')
- grad_qkv_weight: float32 [768, 2304], P('fsdp')
- grad_qkv_bias: float32 [2304], P('fsdp')
- grad_out_weight: float32 [768, 768], P('fsdp')
- grad_out_bias: float32 [768], P('fsdp')
- grad_up_weight: float32 [768, 3072], P('fsdp')
- grad_up_bias: float32 [3072], P('fsdp')
- grad_down_weight: float32 [3072, 768], P('fsdp')
- grad_down_bias: float32 [768], P('fsdp')
All inputs are finite; a program needn't handle non-finite values.
Results may differ from a plain program's by a relative error of at most 0.018.
Values may be sent and summed in bfloat16 or wider, within the bound.
A program may use at most 128 MiB of HBM per device.

v0:
```python
import math
import jax
import jax.numpy as jnp
from jax import lax
from jax.sharding import PartitionSpec as P

HEADS = 12
HEAD = 64
ROT = 16
epsilon = 1e-05
inv_root_two = 1.0 / math.sqrt(2.0)
inv_root_twopi = 1.0 / math.sqrt(2.0 * math.pi)
bf16 = jnp.bfloat16
f32 = jnp.float32


def rotary(tensor, cosine, sine, direction):
    half = ROT // 2
    first = tensor[..., :half]
    second = tensor[..., half:ROT]
    return jnp.concatenate(
        [
            first * cosine - direction * second * sine,
            second * cosine + direction * first * sine,
            tensor[..., ROT:],
        ],
        axis=-1,
    )


def dot(a, b, dims):
    return lax.dot_general(a, b, ((dims[0], dims[1]), ((), ())), preferred_element_type=f32)


NN = ((1,), (0,))
NT = ((1,), (1,))
TN = ((0,), (0,))


def gather_rows(arrays):
    return [lax.all_gather(a, "fsdp", axis=0, tiled=True) for a in arrays]


def scatter_rows(a):
    F = lax.axis_size("fsdp")
    got = lax.all_to_all(a, "fsdp", 0, 0, tiled=True)
    return jnp.sum(got.reshape((F, a.shape[0] // F) + a.shape[1:]).astype(f32), axis=0)


def spread_weights(blocks):
    return lax.all_to_all(blocks, "fsdp", 0, 0, tiled=True)


def return_grads(blocks, own):
    n = lax.axis_size("dp")
    F, W, C = blocks.shape
    R, D = own.shape
    parts = jnp.swapaxes(blocks.reshape(F, n, W // n, C), 0, 1).reshape(n, F * (W // n), C)
    own_parts = own.reshape(n, R // n, D)
    if C == D:
        both = jnp.concatenate([parts, own_parts], axis=1)
        both = jnp.sum(lax.all_to_all(both, "dp", 0, 0, tiled=True).astype(f32), axis=0)
        part, own_part = (both[: F * (W // n)].astype(bf16), both[F * (W // n) :].astype(bf16))
    else:
        part = jnp.sum(lax.all_to_all(parts, "dp", 0, 0, tiled=True).astype(f32), axis=0)
        own_part = jnp.sum(lax.all_to_all(own_parts, "dp", 0, 0, tiled=True).astype(f32), axis=0)
        part, own_part = (part.astype(bf16), own_part.astype(bf16))
    part = lax.all_to_all(part, "fsdp", 0, 0, tiled=True)
    if C == D:
        whole = lax.all_gather(jnp.concatenate([part, own_part], axis=0), "dp", axis=0)
        part_all, own_all = (whole[:, : F * (W // n)], whole[:, F * (W // n) :])
    else:
        part_all = lax.all_gather(part, "dp", axis=0)
        own_all = lax.all_gather(own_part, "dp", axis=0)
    part_all = jnp.swapaxes(part_all.reshape(n, F, W // n, C), 0, 1).reshape(F, W, C)
    return (part_all, own_all.reshape(R, D))


def body(
    tokens,
    ln1_gain,
    ln1_bias,
    ln2_gain,
    ln2_bias,
    qkv_weight,
    qkv_bias,
    out_weight,
    out_bias,
    up_weight,
    up_bias,
    down_weight,
    down_bias,
    cotangent,
):
    rank = lax.axis_index("fsdp")
    F = lax.axis_size("fsdp")
    rows, D = tokens.shape[1:]
    W = D // F
    FFW = down_weight.shape[0]
    NH = max((-(-(g * W % HEAD + W) // HEAD) for g in range(F)))
    WIN = NH * HEAD
    starts = [min(g * W // HEAD, HEADS - NH) * HEAD for g in range(F)]
    start = jnp.minimum(rank * W // HEAD, HEADS - NH) * HEAD
    off = rank * W - start
    S = rows * F
    qkv3 = qkv_weight.reshape(W, 3, D)
    blocks = jnp.stack(
        [
            jnp.concatenate(
                [
                    qkv3[:, 0, s : s + WIN],
                    qkv3[:, 1, s : s + WIN],
                    qkv3[:, 2, s : s + WIN],
                    up_weight[:, g * FFW : (g + 1) * FFW],
                ],
                axis=1,
            )
            for g, s in enumerate(starts)
        ]
    )
    smalls = jnp.concatenate(
        [ln1_gain, ln1_bias, ln2_gain, ln2_bias, out_bias, down_bias, qkv_bias]
    )
    extra = -(-smalls.shape[0] // (16 * D)) * 16
    smalls = jnp.concatenate([smalls, jnp.zeros(extra * D - smalls.shape[0], bf16)])
    (both_all,) = gather_rows([jnp.concatenate([tokens[0], smalls.reshape(extra, D)], axis=0)])
    both_all = both_all.reshape(F, rows + extra, D)
    x_low = both_all[:, :rows].reshape(S, D)
    small_all = both_all[:, rows:].reshape(F, extra * D)
    wall = spread_weights(blocks).reshape(D, 3 * WIN + FFW)
    w_qkv = wall[:, : 3 * WIN]
    w_up = wall[:, 3 * WIN :]
    up_ring = [(i, (i + 1) % F) for i in range(F)]
    down_ring = [(i, (i - 1) % F) for i in range(F)]
    out_prev = lax.ppermute(out_weight, "fsdp", up_ring)
    out_next = lax.ppermute(out_weight, "fsdp", down_ring)
    (grad_out,) = gather_rows([cotangent[0]])
    out_three = jnp.concatenate([out_prev, out_weight, out_next, jnp.zeros((WIN, D), bf16)], axis=0)
    w_out_win = lax.dynamic_slice_in_dim(out_three, W - off, WIN, 0)
    win_col = jnp.arange(WIN, dtype=jnp.int32)
    mine = (win_col >= off) & (win_col < off + W)
    small_all = small_all.astype(f32)
    gain_one, bias_one, gain_two, bias_two, b_out, b_down = [
        small_all[:, i * W : (i + 1) * W].reshape(D) for i in range(6)
    ]
    b_qkv = small_all[:, 6 * W : 9 * W].reshape(3, D)
    b_qkv = lax.dynamic_slice_in_dim(b_qkv, start, WIN, 1).reshape(3 * WIN)
    b_up = up_bias.astype(f32)
    x = x_low.astype(f32)
    center = x - jnp.mean(x, axis=-1, keepdims=True)
    inverse = lax.rsqrt(jnp.mean(center * center, axis=-1, keepdims=True) + epsilon)
    normed = center * inverse
    first_low = (normed * gain_one + bias_one).astype(bf16)
    second_low = (normed * gain_two + bias_two).astype(bf16)
    places = jnp.arange(S, dtype=f32)
    half = ROT // 2
    freq = 10000.0 ** (-(jnp.arange(half, dtype=f32) * 2.0) / ROT)
    angle = places[:, None] * freq[None, :]
    cosine = jnp.cos(angle)[:, None, :]
    sine = jnp.sin(angle)[:, None, :]
    proj = dot(first_low, w_qkv, NN) + b_qkv
    queries = (rotary(proj[:, :WIN].reshape(S, NH, HEAD), cosine, sine, 1.0) * 0.125).astype(bf16)
    keys = rotary(proj[:, WIN : 2 * WIN].reshape(S, NH, HEAD), cosine, sine, 1.0).astype(bf16)
    vals = proj[:, 2 * WIN :].astype(bf16).reshape(S, NH, HEAD)
    q_place = jnp.arange(S, dtype=jnp.int32)
    visible = (q_place[None, :] <= q_place[:, None])[None]
    scores = jnp.einsum("qhd,khd->hqk", queries, keys, preferred_element_type=f32)
    masked = jnp.where(visible, scores, -1e30)
    top = jnp.max(masked, axis=-1, keepdims=True)
    lse = top + jnp.log(jnp.sum(jnp.exp(masked - top), axis=-1, keepdims=True))
    probs = jnp.exp(masked - lse)
    probs_low = probs.astype(bf16)
    attended = jnp.einsum("hqk,khd->qhd", probs_low, vals, preferred_element_type=f32)
    att_low = jnp.where(mine, attended.reshape(S, WIN), 0.0).astype(bf16)
    hidden_pre = dot(second_low, w_up, NN) + b_up
    cdf = 0.5 * (1.0 + lax.erf(hidden_pre * inv_root_two))
    hidden_low = (hidden_pre * cdf).astype(bf16)
    part = dot(att_low, w_out_win, NN) + dot(hidden_low, down_weight, NN)
    branch = scatter_rows(part.astype(bf16))
    grad_hidden = dot(grad_out, down_weight, NT)
    slope = cdf + hidden_pre * jnp.exp(-0.5 * hidden_pre * hidden_pre) * inv_root_twopi
    grad_pre = (grad_hidden * slope).astype(bf16)
    grad_w_down = dot(hidden_low, grad_out, TN)
    grad_w_out_win = dot(att_low, grad_out, TN)
    grad_w_out = lax.dynamic_slice_in_dim(grad_w_out_win, off, W, 0)
    bias_total = jnp.sum(grad_out.astype(f32), axis=0)
    grad_b_up = jnp.sum(grad_pre.astype(f32), axis=0)
    grad_att = dot(grad_out, w_out_win, NT).astype(bf16).reshape(S, NH, HEAD)
    delta = jnp.transpose(jnp.sum(grad_att.astype(f32) * attended, axis=-1))[:, :, None]
    grad_probs = jnp.einsum("qhd,khd->hqk", grad_att, vals, preferred_element_type=f32)
    grad_scores = (probs * (grad_probs - delta)).astype(bf16)
    grad_q = jnp.einsum("hqk,khd->qhd", grad_scores, keys, preferred_element_type=f32)
    grad_k = jnp.einsum("hqk,qhd->khd", grad_scores, queries, preferred_element_type=f32)
    grad_v = jnp.einsum("hqk,qhd->khd", probs_low, grad_att, preferred_element_type=f32)
    grad_proj = jnp.stack(
        [
            rotary(grad_q * 0.125, cosine, sine, -1.0).reshape(S, WIN),
            rotary(grad_k, cosine, sine, -1.0).reshape(S, WIN),
            grad_v.reshape(S, WIN),
        ],
        axis=1,
    )
    grad_proj = jnp.where(mine, grad_proj, 0.0).astype(bf16).reshape(S, 3 * WIN)
    grad_w_qkv = dot(first_low, grad_proj, TN)
    grad_w_up = dot(second_low, grad_pre, TN)
    grad_b_qkv = jnp.sum(grad_proj.astype(f32), axis=0).reshape(3, WIN)
    grad_first = dot(grad_proj, w_qkv, NT)
    grad_second = dot(grad_pre, w_up, NT)
    vectors = [
        jnp.sum(grad_first * normed, axis=0),
        jnp.sum(grad_first, axis=0),
        jnp.sum(grad_second * normed, axis=0),
        jnp.sum(grad_second, axis=0),
    ]
    mixed = grad_first * gain_one + grad_second * gain_two
    b_full = lax.dynamic_update_slice_in_dim(jnp.zeros((3, D), f32), grad_b_qkv, start, 1)
    small_part = jnp.concatenate(
        [v.reshape(F, W) for v in vectors] + [b_full.reshape(F, 3 * W)], axis=1
    )
    mixed_mine = scatter_rows(mixed.astype(bf16))
    small_mine = scatter_rows(small_part)[0]
    own_small = jnp.concatenate(
        [small_mine, lax.dynamic_slice_in_dim(bias_total, rank * W, W, 0), grad_b_up]
    )
    pad = 8 * lax.axis_size("dp")
    own_rows = -(-(W + FFW + -(-own_small.shape[0] // D)) // pad) * pad
    n_small = own_rows - W - FFW
    own_small = jnp.concatenate([own_small, jnp.zeros(n_small * D - own_small.shape[0], f32)])
    grad_blocks = jnp.concatenate([grad_w_qkv, grad_w_up], axis=1).astype(bf16)
    grad_blocks = grad_blocks.reshape(F, W, 3 * WIN + FFW)
    own = jnp.concatenate([grad_w_out, grad_w_down, own_small.reshape(n_small, D)], axis=0).astype(
        bf16
    )
    returned, own = return_grads(grad_blocks, own)
    returned = returned.astype(f32)
    own = own.astype(f32)
    own_small = own[W + FFW :].reshape(n_small * D)
    pieces = [
        [
            returned[g, :, i * WIN + g * W - s : i * WIN + g * W - s + W]
            for g, s in enumerate(starts)
        ]
        for i in range(3)
    ]
    out_w_qkv = jnp.concatenate(pieces[0] + pieces[1] + pieces[2], axis=1)
    out_w_up = jnp.concatenate([returned[g, :, 3 * WIN :] for g in range(F)], axis=1)
    here = rank * rows
    x_own = tokens[0].astype(f32)
    c_own = x_own - jnp.mean(x_own, axis=-1, keepdims=True)
    i_own = lax.rsqrt(jnp.mean(c_own * c_own, axis=-1, keepdims=True) + epsilon)
    n_own = c_own * i_own
    layer_output = (x_own + branch + b_out + b_down).astype(bf16)
    input_grad = cotangent[0].astype(f32) + i_own * (
        mixed_mine
        - jnp.mean(mixed_mine, axis=-1, keepdims=True)
        - n_own * jnp.mean(mixed_mine * n_own, axis=-1, keepdims=True)
    )
    g = [own_small[i * W : (i + 1) * W] for i in range(4)]
    bias_mine = own_small[7 * W : 8 * W]
    return (
        layer_output[None],
        input_grad[None],
        g[0],
        g[1],
        g[2],
        g[3],
        out_w_qkv,
        own_small[4 * W : 7 * W],
        own[:W],
        bias_mine,
        out_w_up,
        own_small[8 * W : 8 * W + FFW],
        own[W : W + FFW],
        bias_mine,
    )


def solution(mesh):
    row = P("fsdp", None)
    vec = P("fsdp")
    act = P("dp", "fsdp", None)
    return jax.shard_map(
        body,
        mesh=mesh,
        in_specs=(act, vec, vec, vec, vec, row, vec, row, vec, row, vec, row, vec, act),
        out_specs=(act, act, vec, vec, vec, vec, row, vec, row, vec, row, vec, row, vec),
        check_vma=False,
    )
```

profile of v0, /device:TPU:0, one launch (start us, length us, event | category | flops | bytes accessed | tf_op | source)
XLA Modules:
  0.0 340.4 jit_solution(5469213770483834597)
XLA Ops:
  8.0 3.0 collective-permute-start
  11.0 3.1 collective-permute-start.1
  14.1 4.8 %concatenate.74 = bf16[12288]{0:T(1024)(128)(2,1)S(1)} concatenate(bf16[96]{0:T(256)(128)(2,1)} %param.15, bf16[96]{0:T(256)(128)(2,1)} %param.16, bf16[96]{0:T(256)(128)(2,1)} %param.17, bf16[96]{0:T(256)(128)(2,1)} %param.18, bf16[96]{0:T(256)(128)(2,1)} %param.22, bf16[96]{0:T(256)(128)(2,1)} %param.26, bf16[288]{0:T(512)(128)(2,1)} %param.20, ...), dimensions={0} | concatenate | bytes 49152 | tf_op jit(solution)/shard_map/concatenate | solution.py:125
  29.4 4.4 %all-to-all-start = ((bf16[8,96,768]{2,1,0:T(8,128)(2,1)}), bf16[8,96,768]{2,1,0:T(8,128)(2,1)}, u32[]{:S(2)}, u32[]{:S(2)}) async-start(bf16[8,96,768]{2,1,0:T(8,128)(2,1)} %fusion.67), calls=%async_computation | async-start | bytes 2359296 | tf_op jit(solution)/shard_map/all_to_all | solution.py:51
  35.0 37.7 %all-gather.8.cloned.1.call-done = bf16[1,1024,768]{2,1,0:T(8,128)(2,1)} async-done(((bf16[1,128,768]{2,1,0:T(8,128)(2,1)}), bf16[1,1024,768]{2,1,0:T(8,128)(2,1)}) %all-gather.8.cloned.1.call-update) | async-done | bytes 1572880 | tf_op jit(solution)/shard_map/all_gather | solution.py:41
  77.3 41.3 %all-gather.6.cloned.1.call-done = bf16[1152,768]{1,0:T(8,128)(2,1)} async-done(((bf16[144,768]{1,0:T(8,128)(2,1)}), bf16[1152,768]{1,0:T(8,128)(2,1)}) %all-gather.6.cloned.1.call-update) | async-done | bytes 1769488 | tf_op jit(solution)/shard_map/all_gather | solution.py:41
  123.4 2.6 add_convert_fusion.4
  126.0 2.4 convolution_add_fusion.1
  132.0 2.4 fusion.69
  134.4 2.4 fusion.29
  136.8 3.3 multiply_convert_fusion
  146.3 2.3 multiply_convert_fusion.1
  150.5 4.1 %fusion.85 = (f32[768]{0:T(1024)S(1)}, f32[768]{0:T(1024)S(1)}, bf16[1024,768]{1,0:T(8,128)(2,1)}, f32[768]{0:T(1024)S(1)}, f32[768]{0:T(1024)S(1)}) fusion(f32[1024]{0:T(1024)S(1)} %get-tuple-element.111, f32[1024]{0:T(1024)S(1)} %get-tuple-element.112, bf16[8,144,768]{2,1,0:T(8,128)(2,1)S(1)} %bitcast.299, f32[768]{0:T(1024)S(1)} %mul.466, ...), kind=kOutput, calls=%fused_computation.216 | convolution fusion | flops 614200320 | bytes 7694336 | tf_op jit(solution)/shard_map/dot_general | solution.py:32
  155.9 4.2 %all-to-all-start.3 = ((f32[8,1,672]{2,1,0:T(1,128)}), f32[8,1,672]{2,1,0:T(1,128)}, u32[]{:S(2)}, u32[]{:S(2)}) async-start(f32[8,1,672]{2,1,0:T(1,128)} %all_to_all.37), calls=%async_computation.3 | async-start | bytes 49152 | tf_op jit(solution)/shard_map/all_to_all | solution.py:46
  160.1 2.6 copy.64
  162.7 3.4 convolution_convert_fusion
  177.4 3.5 %concatenate.91 = bf16[24576]{0:T(1024)(128)(2,1)} concatenate(bf16[672]{0:T(1024)(128)(2,1)} %reduce_sum.192, bf16[96]{0:T(256)(128)(2,1)} %dynamic_slice.41, bf16[384]{0:T(512)(128)(2,1)} %get-tuple-element.123, bf16[23424]{0:T(1024)(128)(2,1)} %broadcast_in_dim.80), dimensions={0} | concatenate | bytes 98304 | tf_op jit(solution)/shard_map/concatenate | solution.py:228
  183.4 27.5 %all_to_all.49 = bf16[4,320,768]{2,1,0:T(8,128)(2,1)} all-to-all(bf16[4,320,768]{2,1,0:T(8,128)(2,1)S(1)} %pad_maximum_fusion), channel_id=1, replica_groups=mesh['dp'=4,'fsdp'=8] {'dp'}, dimensions={0} | all-to-all | bytes 3932160 | tf_op jit(solution)/shard_map/all_to_all | solution.py:62
  213.0 15.6 %all_to_all.50 = bf16[8,24,768]{2,1,0:T(8,128)(2,1)} all-to-all(bf16[8,24,768]{2,1,0:T(8,128)(2,1)S(1)} %bitcast.331), channel_id=1, replica_groups=mesh['dp'=4,'fsdp'=8] {'fsdp'}, dimensions={0} | all-to-all | bytes 589824 | tf_op jit(solution)/shard_map/all_to_all | solution.py:68
  228.6 3.6 %all-to-all-start.2 = ((bf16[8,128,768]{2,1,0:T(8,128)(2,1)}), bf16[8,128,768]{2,1,0:T(8,128)(2,1)S(1)}, u32[]{:S(2)}, u32[]{:S(2)}) async-start(bf16[8,128,768]{2,1,0:T(8,128)(2,1)} %bitcast.326), calls=%async_computation.2 | async-start | bytes 3145728 | tf_op jit(solution)/shard_map/all_to_all | solution.py:46
  233.2 2.7 add_convert_fusion.2
  235.9 32.3 %all-to-all-done.2 = bf16[8,128,768]{2,1,0:T(8,128)(2,1)S(1)} async-done(((bf16[8,128,768]{2,1,0:T(8,128)(2,1)}), bf16[8,128,768]{2,1,0:T(8,128)(2,1)S(1)}, u32[]{:S(2)}, u32[]{:S(2)}) %all-to-all-start.2) | async-done | bytes 1572896 | tf_op jit(solution)/shard_map/all_to_all | solution.py:46
  268.2 4.4 %all-to-all-start.1 = ((bf16[8,128,768]{2,1,0:T(8,128)(2,1)}), bf16[8,128,768]{2,1,0:T(8,128)(2,1)}, u32[]{:S(2)}, u32[]{:S(2)}) async-start(bf16[8,128,768]{2,1,0:T(8,128)(2,1)} %bitcast.313), calls=%async_computation.1 | async-start | bytes 3145728 | tf_op jit(solution)/shard_map/all_to_all | solution.py:46
  274.7 34.3 %all-to-all-done.1 = bf16[8,128,768]{2,1,0:T(8,128)(2,1)} async-done(((bf16[8,128,768]{2,1,0:T(8,128)(2,1)}), bf16[8,128,768]{2,1,0:T(8,128)(2,1)}, u32[]{:S(2)}, u32[]{:S(2)}) %all-to-all-start.1) | async-done | bytes 1572896 | tf_op jit(solution)/shard_map/all_to_all | solution.py:46
  (198 shorter events, 77.9 us)
Async XLA Ops:
  7.2 141.4 %copy-start = (bf16[384,768]{1,0:T(8,128)(2,1)S(1)}, bf16[384,768]{1,0:T(8,128)(2,1)}, u32[]{:S(2)}) copy-start(bf16[384,768]{1,0:T(8,128)(2,1)} %param.25) | copy-start | bytes 1769476
  7.2 65.6 %all-gather.8.cloned.1.call-start = ((), (), s32[]{:S(2)}) async-start(), calls=%async_computation.7 | async-start | bytes 1769472 | tf_op jit(solution)/shard_map/all_gather | solution.py:41
  7.9 110.7 %all-gather.6.cloned.1.call-start = ((), (), s32[]{:S(2)}) async-start(), calls=%async_computation.6 | async-start | bytes 1990656 | tf_op jit(solution)/shard_map/all_gather | solution.py:41
  8.0 67.2 %collective-permute-start = (bf16[96,768]{1,0:T(8,128)(2,1)}, bf16[96,768]{1,0:T(8,128)(2,1)}, u32[]{:S(2)}, u32[]{:S(2)}) collective-permute-start(bf16[96,768]{1,0:T(8,128)(2,1)} %param.21), channel_id=1, source_target_pairs={{0,1},{1,2},{2,3},{3,4},{4,5},{5,6},{6,7},{7,0},{8,9},{9,10},{10,1... | collective-permute-start | bytes 442376 | tf_op jit(solution)/shard_map/ppermute | solution.py:135
  11.0 64.1 %collective-permute-start.1 = (bf16[96,768]{1,0:T(8,128)(2,1)}, bf16[96,768]{1,0:T(8,128)(2,1)}, u32[]{:S(2)}, u32[]{:S(2)}) collective-permute-start(bf16[96,768]{1,0:T(8,128)(2,1)} %param.21), channel_id=1, source_target_pairs={{0,7},{1,0},{2,1},{3,2},{4,3},{5,4},{6,5},{7,6},{8,15},{9,8},{10,9... | collective-permute-start | bytes 442376 | tf_op jit(solution)/shard_map/ppermute | solution.py:136
  20.6 3.0 copy-start.12
  28.0 5.9 %copy-start.18 = (bf16[384]{0:T(512)(128)(2,1)S(1)}, bf16[384]{0:T(512)(128)(2,1)}, u32[]{:S(2)}) copy-start(bf16[384]{0:T(512)(128)(2,1)} %param.24) | copy-start | bytes 2308
  29.4 96.6 %all-to-all-start = ((bf16[8,96,768]{2,1,0:T(8,128)(2,1)}), bf16[8,96,768]{2,1,0:T(8,128)(2,1)}, u32[]{:S(2)}, u32[]{:S(2)}) async-start(bf16[8,96,768]{2,1,0:T(8,128)(2,1)} %fusion.67), calls=%async_computation | async-start | bytes 2359296 | tf_op jit(solution)/shard_map/all_to_all | solution.py:51
  33.8 41.4 %copy-start.14 = (bf16[96,768]{1,0:T(8,128)(2,1)S(1)}, bf16[96,768]{1,0:T(8,128)(2,1)}, u32[]{:S(2)}) copy-start(bf16[96,768]{1,0:T(8,128)(2,1)} %param.21) | copy-start | bytes 442372
  34.0 43.3 %copy-start.19 = (bf16[128]{0:T(256)(128)(2,1)}, bf16[128]{0:T(256)(128)(2,1)S(1)}, u32[]{:S(2)}) copy-start(bf16[128]{0:T(256)(128)(2,1)S(1)} %pad_dynamic-slice_fusion.3) | copy-start | bytes 772
  72.7 2.4 copy-start.2
  118.6 4.2 %copy-start.1 = (bf16[1152,768]{1,0:T(8,128)(2,1)S(1)}, bf16[1152,768]{1,0:T(8,128)(2,1)}, u32[]{:S(2)}) copy-start(bf16[1152,768]{1,0:T(8,128)(2,1)} %all-gather.6.cloned.1.call-done) | copy-start | bytes 5308420
  143.9 2.3 copy-start.6
  150.5 4.1 %copy-start.24 = (bf16[1024,384]{1,0:T(8,128)(2,1)}, bf16[1024,384]{1,0:T(8,128)(2,1)S(1)}, u32[]{:S(2)}) copy-start(bf16[1024,384]{1,0:T(8,128)(2,1)S(1)} %get-tuple-element.124) | copy-start | bytes 2359300
  155.9 19.6 %all-to-all-start.3 = ((f32[8,1,672]{2,1,0:T(1,128)}), f32[8,1,672]{2,1,0:T(1,128)}, u32[]{:S(2)}, u32[]{:S(2)}) async-start(f32[8,1,672]{2,1,0:T(1,128)} %all_to_all.37), calls=%async_computation.3 | async-start | bytes 49152 | tf_op jit(solution)/shard_map/all_to_all | solution.py:46
  175.3 7.2 %copy-start.8 = (bf16[384,768]{1,0:T(8,128)(2,1)S(1)}, bf16[384,768]{1,0:T(8,128)(2,1)}, u32[]{:S(2)}) copy-start(bf16[384,768]{1,0:T(8,128)(2,1)} %fusion.19) | copy-start | bytes 1769476
  213.0 15.6 %copy-start.9 = (bf16[320,768]{1,0:T(8,128)(2,1)}, bf16[320,768]{1,0:T(8,128)(2,1)S(1)}, u32[]{:S(2)}) copy-start(bf16[320,768]{1,0:T(8,128)(2,1)S(1)} %reduce.13) | copy-start | bytes 1474564
  228.6 39.6 %all-to-all-start.2 = ((bf16[8,128,768]{2,1,0:T(8,128)(2,1)}), bf16[8,128,768]{2,1,0:T(8,128)(2,1)S(1)}, u32[]{:S(2)}, u32[]{:S(2)}) async-start(bf16[8,128,768]{2,1,0:T(8,128)(2,1)} %bitcast.326), calls=%async_computation.2 | async-start | bytes 3145728 | tf_op jit(solution)/shard_map/all_to_all | solution.py:46
  268.2 4.5 %slice-start = ((bf16[320,768]{1,0:T(8,128)(2,1)}), bf16[128,768]{1,0:T(8,128)(2,1)S(1)}, s32[]{:S(2)}) async-start(bf16[320,768]{1,0:T(8,128)(2,1)} %copy-done.9), calls=%async_computation.9 | async-start | bytes 393216 | tf_op jit(solution)/shard_map/slice | solution.py:63
  268.2 4.5 %copy-start.10 = (bf16[8,24,768]{2,1,0:T(8,128)(2,1)S(1)}, bf16[8,24,768]{2,1,0:T(8,128)(2,1)}, u32[]{:S(2)}) copy-start(bf16[8,24,768]{2,1,0:T(8,128)(2,1)} %all_to_all.50) | copy-start | bytes 884740
  268.2 40.8 %all-to-all-start.1 = ((bf16[8,128,768]{2,1,0:T(8,128)(2,1)}), bf16[8,128,768]{2,1,0:T(8,128)(2,1)}, u32[]{:S(2)}, u32[]{:S(2)}) async-start(bf16[8,128,768]{2,1,0:T(8,128)(2,1)} %bitcast.313), calls=%async_computation.1 | async-start | bytes 3145728 | tf_op jit(solution)/shard_map/all_to_all | solution.py:46
  272.7 39.0 %all-gather.10.cloned.1.call-start = ((), (), s32[]{:S(2)}) async-start(), calls=%async_computation.8 | async-start | bytes 2457600 | tf_op jit(solution)/shard_map/all_gather | solution.py:70
  274.5 36.2 %copy-start.11 = (bf16[1,128,768]{2,1,0:T(8,128)(2,1)S(1)}, bf16[1,128,768]{2,1,0:T(8,128)(2,1)}, u32[]{:S(2)}) copy-start(bf16[1,128,768]{2,1,0:T(8,128)(2,1)} %param.27) | copy-start | bytes 589828
  316.5 16.8 %copy-start.22 = (f32[96]{0:T(128)}, f32[96]{0:T(128)S(1)}, u32[]{:S(2)}) copy-start(f32[96]{0:T(128)S(1)} %get-tuple-element.176) | copy-start | bytes 1156
  (11 other events, 15.9 us)
Sparse Core Ops, SparseCore 0:
  10.2 62.5 all-gather.7
  75.5 43.0 all-gather.5
  275.6 22.6 all-gather.9
where the time goes:
time: 342 us; the launch traced here: 340 us
  waiting for transfers between devices  146 us (43%)
  local copies, waits for them, and re-layouts  45.6 us (13%)
  blocking collectives  43.1 us (13%)
  matrix products  38.3 us (11%)
  other arithmetic  29.7 us (9%)
  starting transfers between devices  22.9 us (7%)
  between operations  14.6 us (4%)
    all_gather x2, waiting for transfers between devices, gather_rows(): return [lax.all_gather(a, 'fsdp', axis=0, tiled=True) for a in arrays]  79 us
    all_to_all x3, waiting for transfers between devices, scatter_rows(): got = lax.all_to_all(a, 'fsdp', 0, 0, tiled=True)  66.6 us
    all_to_all x1, blocking collectives, return_grads(): lax.all_to_all(both, 'dp', 0, 0, tiled=True).astype(f32)  27.5 us
    dot_general x12, matrix products, dot(): lax.dot_general(a, b, ((dims[0], dims[1]), ((), ())), preferred_element_t...  26.3 us
    all_to_all x1, blocking collectives, return_grads(): part = lax.all_to_all(part, 'fsdp', 0, 0, tiled=True)  15.6 us
    unnamed x72, local copies, waits for them, and re-layouts  14.3 us
    all_to_all x3, starting transfers between devices, scatter_rows(): got = lax.all_to_all(a, 'fsdp', 0, 0, tiled=True)  12.2 us
  transfers between devices with their start and end apart: 9, of which 4 were waited for; matrix products, arithmetic and copies ran while one was open for 15% of the time, Pallas kernels for 0%

commit v1 on v0

--- a/solution.py
+++ b/solution.py
@@ -12,6 +12,19 @@
 inv_root_twopi = 1.0 / math.sqrt(2.0 * math.pi)
 bf16 = jnp.bfloat16
 f32 = jnp.float32
+
+
+def supply_loops(view, k_dim, state):
+    current_value, f_next = (view.shape[:k_dim], view.shape[k_dim + 1 :])
+    return jnp.moveaxis(view.reshape(*current_value, state, -1, *f_next), k_dim, 0)
+
+
+def _pack_zones(work_x, dim_at):
+    work_x = jnp.moveaxis(work_x, 0, dim_at)
+    local_out = work_x.shape
+    return work_x.reshape(
+        *local_out[:dim_at], local_out[dim_at] * local_out[dim_at + 1], *local_out[dim_at + 2 :]
+    )
 
 
 def rotary(tensor, cosine, sine, direction):
@@ -65,7 +78,14 @@
         part = jnp.sum(lax.all_to_all(parts, "dp", 0, 0, tiled=True).astype(f32), axis=0)
         own_part = jnp.sum(lax.all_to_all(own_parts, "dp", 0, 0, tiled=True).astype(f32), axis=0)
         part, own_part = (part.astype(bf16), own_part.astype(bf16))
-    part = lax.all_to_all(part, "fsdp", 0, 0, tiled=True)
+    tall, o_now = (lax.axis_size("fsdp"), lax.axis_index("fsdp"))
+    local_next = supply_loops(part, 0, tall)
+    made = [local_next[o_now]]
+    for dd in range(1, tall):
+        piece_next = local_next[o_now ^ dd]
+        made.append(lax.ppermute(piece_next, "fsdp", [(h, h ^ dd) for h in range(tall)]))
+    local_next = jnp.stack(made, axis=0)[o_now ^ jnp.arange(tall)]
+    part = _pack_zones(local_next, 0)
     if C == D:
         whole = lax.all_gather(jnp.concatenate([part, own_part], axis=0), "dp", axis=0)
         part_all, own_all = (whole[:, : F * (W // n)], whole[:, F * (W // n) :])

time: 342 us -> 318 us (0.930)
  waiting for transfers between devices: 146 us -> 126 us
  starting transfers between devices: 22.9 us -> 39.2 us
  blocking collectives: 43.1 us -> 26.8 us
    all_to_all x3, waiting for transfers between devices: 66.6 us -> 29.2 us  [scatter_rows(): got = lax.all_to_all(a, 'fsdp', 0, 0, tiled=True)]
    ppermute x0 -> x7, waiting for transfers between devices: none -> 16.6 us  [return_grads(): lax.ppermute(piece_next, 'fsdp', [(h, h ^ dd) for h in range(tall)])]
    all_to_all x1 -> x0, blocking collectives: 15.6 us -> none  [return_grads(): part = lax.all_to_all(part, 'fsdp', 0, 0, tiled=True)]
    ppermute x0 -> x7, starting transfers between devices: none -> 15.5 us  [return_grads(): lax.ppermute(piece_next, 'fsdp', [(h, h ^ dd) for h in range(tall)])]
    unnamed x72 -> x96, local copies, waits for them, and re-layouts: 14.3 us -> 9.17 us
    concatenate x1, local copies, waits for them, and re-layouts: 3.53 us -> 0.09 us  [body(): jnp.concatenate([own_small, jnp.zeros(n_small * D - own_small.shape[0], f...]
  transfers between devices with their start and end apart: 9 -> 16, of which waited for: 4 -> 5; matrix products, arithmetic and copies ran while one was open for 15% -> 19% of each run, Pallas kernels for 0% -> 0%
where the time goes in v1:
time: 318 us; the launch traced here: 316 us
  waiting for transfers between devices  126 us (40%)
  local copies, waits for them, and re-layouts  43.4 us (14%)
  matrix products  39.4 us (12%)
  starting transfers between devices  39.2 us (12%)
  other arithmetic  27.3 us (9%)
  blocking collectives  26.8 us (8%)
  between operations  14.7 us (5%)
    all_gather x2, waiting for transfers between devices, gather_rows(): return [lax.all_gather(a, 'fsdp', axis=0, tiled=True) for a in arrays]  79.1 us
    all_to_all x3, waiting for transfers between devices, scatter_rows(): got = lax.all_to_all(a, 'fsdp', 0, 0, tiled=True)  29.2 us
    dot_general x12, matrix products, dot(): lax.dot_general(a, b, ((dims[0], dims[1]), ((), ())), preferred_element_t...  27.5 us
    all_to_all x1, blocking collectives, return_grads(): lax.all_to_all(both, 'dp', 0, 0, tiled=True).astype(f32)  26.8 us
    ppermute x7, waiting for transfers between devices, return_grads(): lax.ppermute(piece_next, 'fsdp', [(h, h ^ dd) for h in range(tall)])  16.6 us
    ppermute x7, starting transfers between devices, return_grads(): lax.ppermute(piece_next, 'fsdp', [(h, h ^ dd) for h in range(tall)])  15.5 us
    all_to_all x3, starting transfers between devices, scatter_rows(): got = lax.all_to_all(a, 'fsdp', 0, 0, tiled=True)  13 us
    unnamed x96, local copies, waits for them, and re-layouts  9.17 us
  transfers between devices with their start and end apart: 16, of which 5 were waited for; matrix products, arithmetic and copies ran while one was open for 19% of the time, Pallas kernels for 0%

profile of v1, /device:TPU:0, one launch (start us, length us, event | category | flops | bytes accessed | tf_op | source)
XLA Modules:
  0.0 316.5 jit_solution(13366992990791433737)
XLA Ops:
  8.0 3.0 collective-permute-start
  11.0 3.1 collective-permute-start.1
  14.1 4.8 %concatenate.74 = bf16[12288]{0:T(1024)(128)(2,1)S(1)} concatenate(bf16[96]{0:T(256)(128)(2,1)} %param.15, bf16[96]{0:T(256)(128)(2,1)} %param.16, bf16[96]{0:T(256)(128)(2,1)} %param.17, bf16[96]{0:T(256)(128)(2,1)} %param.18, bf16[96]{0:T(256)(128)(2,1)} %param.22, bf16[96]{0:T(256)(128)(2,1)} %param.26, bf16[288]{0:T(512)(128)(2,1)} %param.20, ...), dimensions={0} | concatenate | bytes 49152 | tf_op jit(solution)/shard_map/concatenate | solution.py:145
  29.4 4.4 %all-to-all-start = ((bf16[8,96,768]{2,1,0:T(8,128)(2,1)}), bf16[8,96,768]{2,1,0:T(8,128)(2,1)}, u32[]{:S(2)}, u32[]{:S(2)}) async-start(bf16[8,96,768]{2,1,0:T(8,128)(2,1)} %fusion.67), calls=%async_computation | async-start | bytes 2359296 | tf_op jit(solution)/shard_map/all_to_all | solution.py:64
  35.7 37.1 %all-gather.8.cloned.1.call-done = bf16[1,1024,768]{2,1,0:T(8,128)(2,1)} async-done(((bf16[1,128,768]{2,1,0:T(8,128)(2,1)}), bf16[1,1024,768]{2,1,0:T(8,128)(2,1)}) %all-gather.8.cloned.1.call-update) | async-done | bytes 1572880 | tf_op jit(solution)/shard_map/all_gather | solution.py:54
  76.7 42.0 %all-gather.6.cloned.1.call-done = bf16[1152,768]{1,0:T(8,128)(2,1)} async-done(((bf16[144,768]{1,0:T(8,128)(2,1)}), bf16[1152,768]{1,0:T(8,128)(2,1)}) %all-gather.6.cloned.1.call-update) | async-done | bytes 1769488 | tf_op jit(solution)/shard_map/all_gather | solution.py:54
  123.5 2.6 add_convert_fusion.4
  132.1 2.4 fusion.69
  136.9 3.3 %multiply_convert_fusion = bf16[2,1024,1024]{1,2,0:T(8,128)(2,1)S(1)} fusion(f32[2,1024,1024]{1,2,0:T(8,128)S(1)} %get-tuple-element.126, f32[2,1024]{1,0:T(2,128)S(1)} %bitcast.373, f32[2,1024]{1,0:T(2,128)S(1)} %log_add_fusion, pred[1024,1024]{0,1:T(8,128)(4,1)S(1)} %iota_compare_fusion, bf16[1024,2,64]{0,2,1:T(8,128)(2,1)S(1)} %bitcast.372, ...), kind=kOutput, calls=%fused_computation.1 | convolution fusion | flops 278921216 | bytes 14172160 | tf_op jit(solution)/shard_map/qhd,khd->hqk/dot_general | solution.py:210
  151.8 4.1 %fusion.87 = (f32[768]{0:T(1024)S(1)}, f32[768]{0:T(1024)S(1)}, bf16[1024,768]{1,0:T(8,128)(2,1)}, f32[768]{0:T(1024)S(1)}, f32[768]{0:T(1024)S(1)}) fusion(f32[1024]{0:T(1024)S(1)} %get-tuple-element.119, f32[1024]{0:T(1024)S(1)} %get-tuple-element.120, bf16[8,144,768]{2,1,0:T(8,128)(2,1)S(1)} %bitcast.329, f32[768]{0:T(1024)S(1)} %mul.466, ...), kind=kOutput, calls=%fused_computation.236 | convolution fusion | flops 614200320 | bytes 7694336 | tf_op jit(solution)/shard_map/dot_general | solution.py:45
  157.1 3.6 %all-to-all-start.3 = ((f32[8,1,672]{2,1,0:T(1,128)}), f32[8,1,672]{2,1,0:T(1,128)S(1)}, u32[]{:S(2)}, u32[]{:S(2)}) async-start(f32[8,1,672]{2,1,0:T(1,128)} %all_to_all.29), calls=%async_computation.3 | async-start | bytes 49152 | tf_op jit(solution)/shard_map/all_to_all | solution.py:59
  160.7 2.6 copy.64
  163.3 3.4 %convolution_convert_fusion = bf16[8,4,24,384]{3,2,1,0:T(8,128)(2,1)} fusion(bf16[8,4,24,1024]{3,2,1,0:T(8,128)(2,1)} %bitcast.357, bf16[1024,384]{1,0:T(8,128)(2,1)} %copy-done.33), kind=kOutput, calls=%fused_computation.48 | convolution fusion | flops 604274688 | bytes 2949120 | tf_op jit(solution)/shard_map/dot_general | solution.py:45
  176.1 26.8 %all_to_all.37 = bf16[4,320,768]{2,1,0:T(8,128)(2,1)S(1)} all-to-all(bf16[4,320,768]{2,1,0:T(8,128)(2,1)S(1)} %pad_maximum_fusion), channel_id=1, replica_groups=mesh['dp'=4,'fsdp'=8] {'dp'}, dimensions={0} | all-to-all | bytes 3932160 | tf_op jit(solution)/shard_map/all_to_all | solution.py:75
  202.9 5.7 %all-to-all-start.2 = ((bf16[8,128,768]{2,1,0:T(8,128)(2,1)}), bf16[8,128,768]{2,1,0:T(8,128)(2,1)}, u32[]{:S(2)}, u32[]{:S(2)}) async-start(bf16[8,128,768]{2,1,0:T(8,128)(2,1)} %bitcast.355), calls=%async_computation.2 | async-start | bytes 3145728 | tf_op jit(solution)/shard_map/all_to_all | solution.py:59
  208.6 2.6 fusion.96
  214.6 3.8 %add_convert_fusion.2 = bf16[1024,768]{1,0:T(8,128)(2,1)} fusion(f32[1024,768]{1,0:T(8,128)} %fusion.96, bf16[1024,128]{0,1:T(8,128)(2,1)S(1)} %copy-done.9, s32[]{:T(128)S(6)} %select_n.79, bf16[96,768]{1,0:T(8,128)(2,1)} %copy-done.18, bf16[96,768]{1,0:T(8,128)(2,1)S(1)} %copy-done.17, bf16[96,768]{1,0:T(8,128)(2,1)} %copy-done.19, ...), kind=kOutput, calls=%fused_computation.17 | convolution fusion | flops 203685888 | bytes 5423364 | tf_op jit(solution)/shard_map/dot_general | solution.py:45
  219.9 2.9 collective-permute-start.5
  224.3 3.3 %collective-permute-start.7 = (bf16[24,768]{1,0:T(8,128)(2,1)S(1)}, bf16[24,768]{1,0:T(8,128)(2,1)S(1)}, u32[]{:S(2)}, u32[]{:S(2)}) collective-permute-start(bf16[24,768]{1,0:T(8,128)(2,1)S(1)} %get-tuple-element.100), channel_id=1, source_target_pairs={{0,6},{1,7},{2,4},{3,5},{4,2},{5,3},{6,0},{7,1},{8,14},{9,15},{10,... | collective-permute-start | bytes 110600 | tf_op jit(solution)/shard_map/ppermute | solution.py:86
  228.2 8.2 %collective-permute-done.3 = bf16[24,768]{1,0:T(8,128)(2,1)S(1)} collective-permute-done((bf16[24,768]{1,0:T(8,128)(2,1)S(1)}, bf16[24,768]{1,0:T(8,128)(2,1)S(1)}, u32[]{:S(2)}, u32[]{:S(2)}) %collective-permute-start.3) | collective-permute-done | bytes 36896 | tf_op jit(solution)/shard_map/ppermute | solution.py:86
  236.3 4.4 %collective-permute-start.8 = (bf16[24,768]{1,0:T(8,128)(2,1)S(1)}, bf16[24,768]{1,0:T(8,128)(2,1)S(1)}, u32[]{:S(2)}, u32[]{:S(2)}) collective-permute-start(bf16[24,768]{1,0:T(8,128)(2,1)S(1)} %get-tuple-element.99), channel_id=1, source_target_pairs={{0,7},{1,6},{2,5},{3,4},{4,3},{5,2},{6,1},{7,0},{8,15},{9,14},{10,... | collective-permute-start | bytes 110600 | tf_op jit(solution)/shard_map/ppermute | solution.py:86
  241.9 8.4 %collective-permute-done.5 = bf16[24,768]{1,0:T(8,128)(2,1)S(1)} collective-permute-done((bf16[24,768]{1,0:T(8,128)(2,1)S(1)}, bf16[24,768]{1,0:T(8,128)(2,1)S(1)}, u32[]{:S(2)}, u32[]{:S(2)}) %collective-permute-start.5) | collective-permute-done | bytes 36896 | tf_op jit(solution)/shard_map/ppermute | solution.py:86
  251.0 3.7 %all-to-all-start.1 = ((bf16[8,128,768]{2,1,0:T(8,128)(2,1)}), bf16[8,128,768]{2,1,0:T(8,128)(2,1)S(1)}, u32[]{:S(2)}, u32[]{:S(2)}) async-start(bf16[8,128,768]{2,1,0:T(8,128)(2,1)} %bitcast.20), calls=%async_computation.1 | async-start | bytes 3145728 | tf_op jit(solution)/shard_map/all_to_all | solution.py:59
  261.6 29.2 %all-to-all-done.1 = bf16[8,128,768]{2,1,0:T(8,128)(2,1)S(1)} async-done(((bf16[8,128,768]{2,1,0:T(8,128)(2,1)}), bf16[8,128,768]{2,1,0:T(8,128)(2,1)S(1)}, u32[]{:S(2)}, u32[]{:S(2)}) %all-to-all-start.1) | async-done | bytes 1572896 | tf_op jit(solution)/shard_map/all_to_all | solution.py:59
  (240 shorter events, 86.4 us)
Async XLA Ops:
  7.2 142.6 %copy-start = (bf16[384,768]{1,0:T(8,128)(2,1)S(1)}, bf16[384,768]{1,0:T(8,128)(2,1)}, u32[]{:S(2)}) copy-start(bf16[384,768]{1,0:T(8,128)(2,1)} %param.25) | copy-start | bytes 1769476
  7.2 65.6 %all-gather.8.cloned.1.call-start = ((), (), s32[]{:S(2)}) async-start(), calls=%async_computation.6 | async-start | bytes 1769472 | tf_op jit(solution)/shard_map/all_gather | solution.py:54
  7.9 110.7 %all-gather.6.cloned.1.call-start = ((), (), s32[]{:S(2)}) async-start(), calls=%async_computation.5 | async-start | bytes 1990656 | tf_op jit(solution)/shard_map/all_gather | solution.py:54
  8.0 67.2 %collective-permute-start = (bf16[96,768]{1,0:T(8,128)(2,1)}, bf16[96,768]{1,0:T(8,128)(2,1)S(1)}, u32[]{:S(2)}, u32[]{:S(2)}) collective-permute-start(bf16[96,768]{1,0:T(8,128)(2,1)} %param.21), channel_id=1, source_target_pairs={{0,1},{1,2},{2,3},{3,4},{4,5},{5,6},{6,7},{7,0},{8,9},{9,10},{10,1... | collective-permute-start | bytes 442376 | tf_op jit(solution)/shard_map/ppermute | solution.py:155
  11.0 64.2 %collective-permute-start.1 = (bf16[96,768]{1,0:T(8,128)(2,1)}, bf16[96,768]{1,0:T(8,128)(2,1)S(1)}, u32[]{:S(2)}, u32[]{:S(2)}) collective-permute-start(bf16[96,768]{1,0:T(8,128)(2,1)} %param.21), channel_id=1, source_target_pairs={{0,7},{1,0},{2,1},{3,2},{4,3},{5,4},{6,5},{7,6},{8,15},{9,8},{10,9... | collective-permute-start | bytes 442376 | tf_op jit(solution)/shard_map/ppermute | solution.py:156
  28.0 5.9 %copy-start.26 = (bf16[384]{0:T(512)(128)(2,1)S(1)}, bf16[384]{0:T(512)(128)(2,1)}, u32[]{:S(2)}) copy-start(bf16[384]{0:T(512)(128)(2,1)} %param.24) | copy-start | bytes 2308
  29.4 96.7 %all-to-all-start = ((bf16[8,96,768]{2,1,0:T(8,128)(2,1)}), bf16[8,96,768]{2,1,0:T(8,128)(2,1)}, u32[]{:S(2)}, u32[]{:S(2)}) async-start(bf16[8,96,768]{2,1,0:T(8,128)(2,1)} %fusion.67), calls=%async_computation | async-start | bytes 2359296 | tf_op jit(solution)/shard_map/all_to_all | solution.py:64
  33.9 41.3 %copy-start.16 = (bf16[96,768]{1,0:T(8,128)(2,1)S(1)}, bf16[96,768]{1,0:T(8,128)(2,1)}, u32[]{:S(2)}) copy-start(bf16[96,768]{1,0:T(8,128)(2,1)} %param.21) | copy-start | bytes 442372
  34.6 42.0 %copy-start.27 = (bf16[128]{0:T(256)(128)(2,1)}, bf16[128]{0:T(256)(128)(2,1)S(1)}, u32[]{:S(2)}) copy-start(bf16[128]{0:T(256)(128)(2,1)S(1)} %pad_dynamic-slice_fusion.3) | copy-start | bytes 772
  157.1 18.1 %all-to-all-start.3 = ((f32[8,1,672]{2,1,0:T(1,128)}), f32[8,1,672]{2,1,0:T(1,128)S(1)}, u32[]{:S(2)}, u32[]{:S(2)}) async-start(f32[8,1,672]{2,1,0:T(1,128)} %all_to_all.29), calls=%async_computation.3 | async-start | bytes 49152 | tf_op jit(solution)/shard_map/all_to_all | solution.py:59
  202.9 48.1 %all-to-all-start.2 = ((bf16[8,128,768]{2,1,0:T(8,128)(2,1)}), bf16[8,128,768]{2,1,0:T(8,128)(2,1)}, u32[]{:S(2)}, u32[]{:S(2)}) async-start(bf16[8,128,768]{2,1,0:T(8,128)(2,1)} %bitcast.355), calls=%async_computation.2 | async-start | bytes 3145728 | tf_op jit(solution)/shard_map/all_to_all | solution.py:59
  211.8 6.6 %copy-start.10 = (bf16[320,768]{1,0:T(8,128)(2,1)}, bf16[320,768]{1,0:T(8,128)(2,1)S(1)}, u32[]{:S(2)}) copy-start(bf16[320,768]{1,0:T(8,128)(2,1)S(1)} %reduce.13) | copy-start | bytes 1474564
  212.6 11.7 %collective-permute-start.2 = (bf16[24,768]{1,0:T(8,128)(2,1)S(1)}, bf16[24,768]{1,0:T(8,128)(2,1)S(1)}, u32[]{:S(2)}, u32[]{:S(2)}) collective-permute-start(bf16[24,768]{1,0:T(8,128)(2,1)S(1)} %get-tuple-element.105), channel_id=1, source_target_pairs={{0,1},{1,0},{2,3},{3,2},{4,5},{5,4},{6,7},{7,6},{8,9},{9,8},{10,11... | collective-permute-start | bytes 110600 | tf_op jit(solution)/shard_map/ppermute | solution.py:86
  218.4 17.9 %collective-permute-start.3 = (bf16[24,768]{1,0:T(8,128)(2,1)S(1)}, bf16[24,768]{1,0:T(8,128)(2,1)S(1)}, u32[]{:S(2)}, u32[]{:S(2)}) collective-permute-start(bf16[24,768]{1,0:T(8,128)(2,1)S(1)} %get-tuple-element.104), channel_id=1, source_target_pairs={{0,2},{1,3},{2,0},{3,1},{4,6},{5,7},{6,4},{7,5},{8,10},{9,11},{10,... | collective-permute-start | bytes 110600 | tf_op jit(solution)/shard_map/ppermute | solution.py:86
  219.9 21.4 %collective-permute-start.4 = (bf16[24,768]{1,0:T(8,128)(2,1)S(1)}, bf16[24,768]{1,0:T(8,128)(2,1)S(1)}, u32[]{:S(2)}, u32[]{:S(2)}) collective-permute-start(bf16[24,768]{1,0:T(8,128)(2,1)S(1)} %get-tuple-element.103), channel_id=1, source_target_pairs={{0,3},{1,2},{2,1},{3,0},{4,7},{5,6},{6,5},{7,4},{8,11},{9,10},{10,... | collective-permute-start | bytes 110600 | tf_op jit(solution)/shard_map/ppermute | solution.py:86
  219.9 30.5 %collective-permute-start.5 = (bf16[24,768]{1,0:T(8,128)(2,1)S(1)}, bf16[24,768]{1,0:T(8,128)(2,1)S(1)}, u32[]{:S(2)}, u32[]{:S(2)}) collective-permute-start(bf16[24,768]{1,0:T(8,128)(2,1)S(1)} %get-tuple-element.102), channel_id=1, source_target_pairs={{0,4},{1,5},{2,6},{3,7},{4,0},{5,1},{6,2},{7,3},{8,12},{9,13},{10,... | collective-permute-start | bytes 110600 | tf_op jit(solution)/shard_map/ppermute | solution.py:86
  222.8 32.0 %collective-permute-start.6 = (bf16[24,768]{1,0:T(8,128)(2,1)}, bf16[24,768]{1,0:T(8,128)(2,1)S(1)}, u32[]{:S(2)}, u32[]{:S(2)}) collective-permute-start(bf16[24,768]{1,0:T(8,128)(2,1)} %get-tuple-element.101), channel_id=1, source_target_pairs={{0,5},{1,4},{2,7},{3,6},{4,1},{5,0},{6,3},{7,2},{8,13},{9,12},{10,... | collective-permute-start | bytes 110600 | tf_op jit(solution)/shard_map/ppermute | solution.py:86
  224.3 31.1 %collective-permute-start.7 = (bf16[24,768]{1,0:T(8,128)(2,1)S(1)}, bf16[24,768]{1,0:T(8,128)(2,1)S(1)}, u32[]{:S(2)}, u32[]{:S(2)}) collective-permute-start(bf16[24,768]{1,0:T(8,128)(2,1)S(1)} %get-tuple-element.100), channel_id=1, source_target_pairs={{0,6},{1,7},{2,4},{3,5},{4,2},{5,3},{6,0},{7,1},{8,14},{9,15},{10,... | collective-permute-start | bytes 110600 | tf_op jit(solution)/shard_map/ppermute | solution.py:86
  236.3 19.7 %collective-permute-start.8 = (bf16[24,768]{1,0:T(8,128)(2,1)S(1)}, bf16[24,768]{1,0:T(8,128)(2,1)S(1)}, u32[]{:S(2)}, u32[]{:S(2)}) collective-permute-start(bf16[24,768]{1,0:T(8,128)(2,1)S(1)} %get-tuple-element.99), channel_id=1, source_target_pairs={{0,7},{1,6},{2,5},{3,4},{4,3},{5,2},{6,1},{7,0},{8,15},{9,14},{10,... | collective-permute-start | bytes 110600 | tf_op jit(solution)/shard_map/ppermute | solution.py:86
  251.0 7.2 %slice-start = ((bf16[320,768]{1,0:T(8,128)(2,1)}), bf16[128,768]{1,0:T(8,128)(2,1)S(1)}, s32[]{:S(2)}) async-start(bf16[320,768]{1,0:T(8,128)(2,1)} %copy-done.10), calls=%async_computation.8 | async-start | bytes 393216 | tf_op jit(solution)/shard_map/slice | solution.py:76
  251.0 39.8 %all-to-all-start.1 = ((bf16[8,128,768]{2,1,0:T(8,128)(2,1)}), bf16[8,128,768]{2,1,0:T(8,128)(2,1)S(1)}, u32[]{:S(2)}, u32[]{:S(2)}) async-start(bf16[8,128,768]{2,1,0:T(8,128)(2,1)} %bitcast.20), calls=%async_computation.1 | async-start | bytes 3145728 | tf_op jit(solution)/shard_map/all_to_all | solution.py:59
  254.7 37.3 %all-gather.10.cloned.1.call-start = ((), (), s32[]{:S(2)}) async-start(), calls=%async_computation.7 | async-start | bytes 2457600 | tf_op jit(solution)/shard_map/all_gather | solution.py:90
  261.4 29.7 %copy-start.11 = (bf16[1,128,768]{2,1,0:T(8,128)(2,1)S(1)}, bf16[1,128,768]{2,1,0:T(8,128)(2,1)}, u32[]{:S(2)}) copy-start(bf16[1,128,768]{2,1,0:T(8,128)(2,1)} %param.27) | copy-start | bytes 589828
  299.4 10.1 %copy-start.31 = (f32[96]{0:T(128)}, f32[96]{0:T(128)S(1)}, u32[]{:S(2)}) copy-start(f32[96]{0:T(128)S(1)} %get-tuple-element.184) | copy-start | bytes 1156
  (27 other events, 59.0 us)
Sparse Core Ops, SparseCore 0:
  10.2 62.5 all-gather.7
  75.5 43.0 all-gather.5
  259.1 22.4 all-gather.9
